TPU v7x, 128 devices: a whole 4x4x4 slice. The times are simulated.
128 devices in a mesh: frame: 8 (over x_hi, z), pos: 16 (over y, x_lo, core).
Axes of the slice: x: 4 (x_hi: 2, x_lo: 2; x = x_hi * 2 + x_lo), y: 4, z: 4, core: 2. Of those that a mesh axis runs over, the one named last changes fastest.
Arguments:
- latents: bfloat16 [256, 1024, 256], P('frame', 'pos'), as said below
- gain_one: float32 [256], replicated, may hold values from 0.5 to 1.5
- query_one: bfloat16 [256, 256], replicated, as said below
- key_one: bfloat16 [256, 256], replicated, as said below
- value_one: bfloat16 [256, 256], replicated, may hold values from -0.375 to 0.375
- out_one: bfloat16 [256, 256], replicated, may hold values from -0.75 to 0.75
- gain_two: float32 [256], replicated, may hold values from 0.5 to 1.5
- query_two: bfloat16 [256, 256], replicated, as said below
- key_two: bfloat16 [256, 256], replicated, as said below
- value_two: bfloat16 [256, 256], replicated, may hold values from -0.375 to 0.375
- out_two: bfloat16 [256, 256], replicated, may hold values from -0.75 to 0.75
Outputs:
- decoded: bfloat16 [256, 1024, 256], P('frame', 'pos')
Inputs may be any that keep to these rules, and one draw needn't show every extreme that they name: `latents`: latent features of the video. `query_one`: A projection of the spatial block. `key_one`: A projection of the spatial block. `query_two`: A projection of the temporal block. `key_two`: A projection of the temporal block.
All inputs are finite; a program needn't handle non-finite values.
Results may differ from a plain program's by a relative error of at most 0.015.
The roundings to bfloat16 on the way count: a program that leaves them out, or rounds other values in their place, can miss the bound.
Values may be sent and summed in bfloat16 or wider, within the bound.
A program may use at most 320 MiB of HBM per device.

v0:
```python
import jax
import jax.numpy as jnp
from jax import lax
from jax.sharding import PartitionSpec as P

HEADS = 4


def broadcast(value, axis, source):
    kept = jnp.where(lax.axis_index(axis) == source, value, 0).astype(value.dtype)
    return lax.psum(kept, axis)


def normed(values, gain):
    wide = values.astype(jnp.float32)
    factor = lax.rsqrt(jnp.mean(wide * wide, axis=-1, keepdims=True) + 1e-06)
    return (wide * factor * gain).astype(jnp.bfloat16)


def project(values, weight):
    flat = values.reshape(-1, values.shape[-1])
    result = jnp.dot(flat, weight, preferred_element_type=jnp.float32).astype(jnp.bfloat16)
    return result.reshape(values.shape[:-1] + (weight.shape[1],))


def heads_of(values):
    return values.reshape(values.shape[:-1] + (HEADS, values.shape[-1] // HEADS))


def soft_step(carry, query, keys, vals, score_form, value_form):
    highest, totals, summed = carry
    scale = query.shape[-1] ** (-0.5)
    scores = jnp.einsum(score_form, query, keys, preferred_element_type=jnp.float32) * scale
    new_high = jnp.maximum(highest, jnp.max(scores, axis=-1))
    keep = jnp.exp(highest - new_high)
    weights = jnp.exp(scores - new_high[..., None])
    totals = totals * keep + jnp.sum(weights, axis=-1)
    summed = summed * keep[..., None] + jnp.einsum(
        value_form, weights.astype(jnp.bfloat16), vals, preferred_element_type=jnp.float32
    )
    return (new_high, totals, summed)


def empty_carry(lead, depth):
    return (
        jnp.full(lead, -1e30, jnp.float32),
        jnp.zeros(lead, jnp.float32),
        jnp.zeros(lead + (depth,), jnp.float32),
    )


def shards(
    latents,
    gain_one,
    query_one,
    key_one,
    value_one,
    out_one,
    gain_two,
    query_two,
    key_two,
    value_two,
    out_two,
):
    frames, places, width = latents.shape
    depth = width // HEADS
    normed_one = normed(latents, gain_one)
    q_one = heads_of(project(normed_one, query_one))
    k_one = project(normed_one, key_one)
    v_one = project(normed_one, value_one)
    first_keys, first_vals = (k_one[0], v_one[0])
    first_keys, first_vals = (broadcast(first_keys, "frame", 0), broadcast(first_vals, "frame", 0))
    first_keys, first_vals = (
        lax.all_gather(first_keys, "pos", axis=0, tiled=True),
        lax.all_gather(first_vals, "pos", axis=0, tiled=True),
    )
    carry = empty_carry((frames, HEADS, places), depth)
    carry = soft_step(
        carry, q_one, heads_of(first_keys), heads_of(first_vals), "fphd,khd->fhpk", "fhpk,khd->fhpd"
    )
    pieces = (
        lax.all_gather(k_one, "pos", axis=1, tiled=True),
        lax.all_gather(v_one, "pos", axis=1, tiled=True),
    )
    carry = soft_step(
        carry, q_one, heads_of(pieces[0]), heads_of(pieces[1]), "fphd,fkhd->fhpk", "fhpk,fkhd->fhpd"
    )
    attended_one = (
        (carry[2] / carry[1][..., None])
        .transpose(0, 2, 1, 3)
        .reshape(frames, places, width)
        .astype(jnp.bfloat16)
    )
    mixed_one = jnp.dot(
        attended_one.reshape(-1, width), out_one, preferred_element_type=jnp.float32
    ).reshape(frames, places, width)
    middle = (latents.astype(jnp.float32) + mixed_one).astype(jnp.bfloat16)
    normed_two = normed(middle, gain_two)
    q_two = heads_of(project(normed_two, query_two))
    carry_two = empty_carry((places, HEADS, frames), depth)
    k_two = project(normed_two, key_two)
    v_two = project(normed_two, value_two)
    pieces = (
        lax.all_gather(k_two, "frame", axis=0, tiled=True),
        lax.all_gather(v_two, "frame", axis=0, tiled=True),
    )
    carry_two = soft_step(
        carry_two,
        q_two,
        heads_of(pieces[0]),
        heads_of(pieces[1]),
        "fphd,kphd->phfk",
        "phfk,kphd->phfd",
    )
    attended_two = (
        (carry_two[2] / carry_two[1][..., None])
        .transpose(2, 0, 1, 3)
        .reshape(frames, places, width)
        .astype(jnp.bfloat16)
    )
    mixed_two = jnp.dot(
        attended_two.reshape(-1, width), out_two, preferred_element_type=jnp.float32
    ).reshape(frames, places, width)
    return (middle.astype(jnp.float32) + mixed_two).astype(jnp.bfloat16)


def solution(mesh):
    return jax.shard_map(
        shards,
        mesh=mesh,
        in_specs=(P("frame", "pos", None), P(), P(), P(), P(), P(), P(), P(), P(), P(), P()),
        out_specs=P("frame", "pos", None),
        check_vma=False,
    )
```

profile of v0, /device:TPU:1, one launch (start us, length us, event | category | flops | bytes accessed | tf_op | source)
XLA Modules:
  0.0 649.6 jit_solution(16036912624553404310)
XLA Ops:
  7.4 1.6 fusion.27
  9.0 1.6 fusion.29
  10.6 1.3 convolution_convert_fusion.3
  11.9 1.3 convolution_convert_fusion.5
  13.3 0.7 slice_select_fusion
  14.0 0.2 copy-done.3
  14.3 0.3 all-gather.5.cloned.1.call-update
  14.6 1.6 copy.78
  16.3 0.4 convolution_convert_fusion.4
  16.7 0.9 reshape_reshape.6
  17.6 1.9 copy.71
  19.5 174.5 %all-reduce.3.cloned.1.call-done = (bf16[64,256]{1,0:T(8,128)(2,1)}, bf16[64,256]{1,0:T(8,128)(2,1)}) async-done(((bf16[64,256]{1,0:T(8,128)(2,1)}, bf16[64,256]{1,0:T(8,128)(2,1)}), (bf16[64,256]{1,0:T(8,128)(2,1)}, bf16[64,256]{1,0:T(8,128)(2,1)})) %all-reduce.3.cloned.1.call-update) | async-done | bytes 65552 | tf_op jit(solution)/shard_map/psum | solution.py:11
  194.0 30.8 %all_gather.18 = bf16[1024,256]{1,0:T(8,128)(2,1)S(1)} all-gather(bf16[64,256]{1,0:T(8,128)(2,1)} %get-tuple-element.6), channel_id=1, replica_groups=mesh['frame'=8,'pos'=16] {'pos'}, dimensions={0}, use_global_device_ids=true | all-gather | bytes 557056 | tf_op jit(solution)/shard_map/all_gather | solution.py:74
  224.8 0.2 copy.70
  225.0 20.4 %all_gather.19 = bf16[1024,256]{1,0:T(8,128)(2,1)} all-gather(bf16[64,256]{1,0:T(8,128)(2,1)} %get-tuple-element.5), channel_id=1, replica_groups=mesh['frame'=8,'pos'=16] {'pos'}, dimensions={0}, use_global_device_ids=true | all-gather | bytes 557056 | tf_op jit(solution)/shard_map/all_gather | solution.py:75
  245.4 1.2 copy.72
  246.6 14.7 %fusion.50 = f32[4,1024,2048]{1,2,0} fusion(bf16[4,64,2048]{1,2,0:T(8,128)(2,1)} %bitcast.115, bf16[1024,4,64]{0,2,1:T(8,128)(2,1)S(1)} %bitcast.122), kind=kOutput, calls=%fused_computation.75 | convolution fusion | flops 1073741824 | bytes 35127296
  261.3 12.1 %bitcast_reduce_fusion = f32[32,4,64]{2,0,1:T(8,128)S(1)} fusion(f32[4,1024,32,64]{1,3,2,0:T(8,128)} %bitcast.103), kind=kLoop, calls=%fused_computation.1 | loop fusion | flops 16769024 | bytes 33587200 | tf_op jit(solution)/shard_map/reduce_max | solution.py:34
  273.5 22.5 %copy.73 = bf16[32,1024,256]{1,2,0:T(8,128)(2,1)} copy(bf16[32,1024,256]{2,1,0:T(8,128)(2,1)} %all-gather.5.cloned.1.call-done) | data formatting | bytes 33554432 | tf_op jit(solution)/shard_map/all_gather | solution.py:82
  296.1 16.5 %multiply_reduce_fusion = (f32[32,4,64]{2,1,0:T(4,128)S(1)}, f32[32,4,64,1024]{3,2,1,0:T(8,128)}) fusion(bf16[32,1024,4,64]{1,3,2,0:T(8,128)(2,1)} %bitcast.106, bf16[32,64,4,64]{3,2,1,0:T(4,128)(2,1)S(1)} %reshape_reshape.6), kind=kOutput, calls=%fused_computation.4 | convolution fusion | flops 1090510848 | bytes 51412992 | tf_op jit(solution)/shard_map/fphd,fkhd->fhpk/dot_general | solution.py:33
  312.6 14.8 %fusion.3 = f32[32,4,64]{2,0,1:T(8,128)S(1)} fusion(f32[4,1024,32,64]{1,3,2,0:T(8,128)} %bitcast.104, f32[32,4,64]{2,0,1:T(8,128)S(1)} %get-tuple-element.15), kind=kLoop, calls=%fused_computation.7 | loop fusion | flops 25157632 | bytes 33619968 | tf_op jit(solution)/shard_map/reduce_sum | solution.py:37
  327.4 5.3 copy-done.1
  332.7 9.8 %fusion.1 = (f32[32,4,64]{2,1,0:T(4,128)S(1)}, bf16[32,4,64,1024]{3,2,1,0:T(8,128)(2,1)}) fusion(f32[32,4,64,1024]{3,2,1,0:T(8,128)S(1)} %copy-done.1, f32[32,4,64]{2,1,0:T(4,128)S(1)} %copy.77), kind=kLoop, calls=%fused_computation.5 | loop fusion | flops 33546240 | bytes 50397184 | tf_op jit(solution)/shard_map/reduce_sum | solution.py:37
  342.6 16.1 %fusion.5 = f32[4,64,32,64]{3,1,2,0:T(8,128)} fusion(bf16[1024,4,64,1]{0,2,3,1:T(8,128)(2,1)S(1)} %bitcast.121, f32[4,1024,32,64]{1,3,2,0:T(8,128)} %bitcast.105, f32[32,4,64]{2,0,1:T(8,128)S(1)} %get-tuple-element.15), kind=kOutput, calls=%fused_computation.9 | convolution fusion | flops 1098907648 | bytes 36208640 | tf_op jit(solution)/shard_map/fhpk,khd->fhpd/dot_general | solution.py:38
  358.7 23.2 %copy.79 = bf16[32,1024,256]{1,2,0:T(8,128)(2,1)} copy(bf16[32,1024,256]{2,0,1:T(8,128)(2,1)} %all-gather.7.cloned.1.call-done) | data formatting | bytes 33554432 | tf_op jit(solution)/shard_map/all_gather | solution.py:83
  382.0 15.0 %fusion.19 = bf16[32,64,4,64]{1,3,0,2:T(8,128)(2,1)} fusion(f32[4,64,32,64]{3,1,2,0:T(8,128)} %fusion.5, bf16[32,1024,4,64]{1,3,2,0:T(8,128)(2,1)} %bitcast.108, bf16[32,4,64,1024]{3,2,1,0:T(8,128)(2,1)} %get-tuple-element.10, f32[32,64,4]{1,0,2:T(8,128)S(1)} %get-tuple-element.7, f32[32,64,4]{1,0,2:T(8,128)S(1)} %get-tuple-element.8, ...), kind=kOutput, calls=%fused_computation.25 | convolution fusion | flops 1076363264 | bytes 36798464 | tf_op jit(solution)/shard_map/fhpk,fkhd->fhpd/dot_general | solution.py:38
  397.0 3.1 copy.84
  400.1 2.2 convert_element_type.74
  402.3 1.8 fusion.31
  404.1 0.9 copy-done.4
  405.1 0.3 fusion.33
  405.4 1.4 convolution_convert_fusion.1
  406.9 1.5 convolution_convert_fusion
  408.5 0.4 convolution_convert_fusion.2
  408.9 0.9 reshape_reshape.7
  409.8 99.1 %all-gather.9.cloned.1.call-done = bf16[256,64,256]{2,1,0:T(8,128)(2,1)} async-done(((bf16[32,64,256]{2,1,0:T(8,128)(2,1)}), bf16[256,64,256]{2,1,0:T(8,128)(2,1)}) %all-gather.9.cloned.1.call-update) | async-done | bytes 8388624 | tf_op jit(solution)/shard_map/all_gather | solution.py:104
  508.8 13.0 %copy.85 = bf16[256,64,256]{0,2,1:T(8,128)(2,1)} copy(bf16[256,64,256]{2,1,0:T(8,128)(2,1)} %all-gather.9.cloned.1.call-done) | data formatting | bytes 16777216 | tf_op jit(solution)/shard_map/all_gather | solution.py:104
  521.8 5.7 multiply_reduce_fusion.1
  527.5 0.1 multiply_bitcast_fusion
  527.6 3.1 copy-done.2
  530.7 2.8 fusion.12
  533.6 0.1 bitcast_add_fusion.3
  533.6 82.9 %all-gather.11.cloned.1.call-done = bf16[256,64,256]{2,1,0:T(8,128)(2,1)} async-done(((bf16[32,64,256]{2,1,0:T(8,128)(2,1)}), bf16[256,64,256]{2,1,0:T(8,128)(2,1)}) %all-gather.11.cloned.1.call-update) | async-done | bytes 8388624 | tf_op jit(solution)/shard_map/all_gather | solution.py:105
  616.5 12.9 %copy.87 = bf16[256,64,256]{0,2,1:T(8,128)(2,1)} copy(bf16[256,64,256]{2,1,0:T(8,128)(2,1)} %all-gather.11.cloned.1.call-done) | data formatting | bytes 16777216 | tf_op jit(solution)/shard_map/all_gather | solution.py:105
  629.4 8.0 %fusion.17 = bf16[32,64,4,64]{3,0,2,1:T(8,128)(2,1)S(1)} fusion(f32[32,64,4]{0,2,1:T(4,128)S(1)} %bitcast_add_fusion.3, f32[32,64,4]{0,2,1:T(4,128)S(1)} %get-tuple-element.11, bf16[256,64,4,64]{0,3,2,1:T(8,128)(2,1)} %bitcast.116, f32[64,4,32,256]{3,2,1,0:T(8,128)} %copy-done.2, f32[64,4,32]{2,1,0:T(4,128)S(1)} %get-tuple-element.12), kind=kOutput, calls=%fused_computation.22 | convolution fusion | flops 276299776 | bytes 17924096 | tf_op jit(solution)/shard_map/phfk,kphd->phfd/dot_general | solution.py:38
  637.4 1.1 copy.88
  638.5 1.4 convert_element_type.83
  639.9 2.6 fusion.34
  (36 shorter events, 0.4 us)
Async XLA Ops:
  7.4 394.9 %copy-start = (bf16[256,256]{1,0:T(8,128)(2,1)S(1)}, bf16[256,256]{1,0:T(8,128)(2,1)}, u32[]{:S(2)}) copy-start(bf16[256,256]{1,0:T(8,128)(2,1)} %param.16) | copy-start | bytes 393220
  7.4 8.9 %copy-start.6 = (bf16[256,256]{1,0:T(8,128)(2,1)S(1)}, bf16[256,256]{1,0:T(8,128)(2,1)}, u32[]{:S(2)}) copy-start(bf16[256,256]{1,0:T(8,128)(2,1)} %param.13) | copy-start | bytes 393220
  7.4 186.6 %all-reduce.3.cloned.1.call-start = ((), (), s32[]{:S(2)}) async-start(), calls=%async_computation.4 | async-start | bytes 131072 | tf_op jit(solution)/shard_map/psum | solution.py:11
  13.3 1.0 copy-start.3
  14.0 259.5 %all-gather.5.cloned.1.call-start = ((), (), s32[]{:S(2)}) async-start(), calls=%async_computation | async-start | bytes 17825792 | tf_op jit(solution)/shard_map/all_gather | solution.py:82
  14.6 344.1 %all-gather.7.cloned.1.call-start = ((), (), s32[]{:S(2)}) async-start(), calls=%async_computation.1 | async-start | bytes 17825792 | tf_op jit(solution)/shard_map/all_gather | solution.py:83
  16.2 492.6 %all-gather.9.cloned.1.call-start = ((), (), s32[]{:S(2)}) async-start(), calls=%async_computation.2 | async-start | bytes 9437184 | tf_op jit(solution)/shard_map/all_gather | solution.py:104
  312.6 20.2 %copy-start.1 = (f32[32,4,64,1024]{3,2,1,0:T(8,128)S(1)}, f32[32,4,64,1024]{3,2,1,0:T(8,128)}, u32[]{:S(2)}) copy-start(f32[32,4,64,1024]{3,2,1,0:T(8,128)} %get-tuple-element.17) | copy-start | bytes 100663296
  382.0 20.3 %copy-start.5 = (bf16[32,64,256]{2,1,0:T(8,128)(2,1)S(1)}, bf16[32,64,256]{2,1,0:T(8,128)(2,1)}, u32[]{:S(2)}) copy-start(bf16[32,64,256]{2,1,0:T(8,128)(2,1)} %param.11) | copy-start | bytes 3145732
  397.0 8.1 %copy-start.11 = (f32[256]{0:T(256)S(1)}, f32[256]{0:T(256)}, u32[]{:S(2)}) copy-start(f32[256]{0:T(256)} %param.17) | copy-start | bytes 3076
  397.0 8.4 %copy-start.7 = (bf16[256,256]{1,0:T(8,128)(2,1)S(1)}, bf16[256,256]{1,0:T(8,128)(2,1)}, u32[]{:S(2)}) copy-start(bf16[256,256]{1,0:T(8,128)(2,1)} %param.19) | copy-start | bytes 393220
  397.0 9.9 %copy-start.8 = (bf16[256,256]{1,0:T(8,128)(2,1)S(1)}, bf16[256,256]{1,0:T(8,128)(2,1)}, u32[]{:S(2)}) copy-start(bf16[256,256]{1,0:T(8,128)(2,1)} %param.20) | copy-start | bytes 393220
  402.3 6.2 copy-start.9
  404.1 1.0 copy-start.4
  406.9 209.7 %all-gather.11.cloned.1.call-start = ((), (), s32[]{:S(2)}) async-start(), calls=%async_computation.3 | async-start | bytes 9437184 | tf_op jit(solution)/shard_map/all_gather | solution.py:105
  527.5 3.2 copy-start.2
  629.4 10.5 %copy-start.10 = (bf16[256,256]{1,0:T(8,128)(2,1)S(1)}, bf16[256,256]{1,0:T(8,128)(2,1)}, u32[]{:S(2)}) copy-start(bf16[256,256]{1,0:T(8,128)(2,1)} %param.21) | copy-start | bytes 393220
Sparse Core Ops, SparseCore 0:
  14.1 179.8 all-reduce.2
  407.0 101.8 all-gather.8
  511.5 105.0 all-gather.10
Sparse Core Ops, SparseCore 1:
  16.2 95.5 all-gather.4
  113.5 94.1 all-gather.6
where the time goes:
time: 652 us; the launch traced here: 650 us
  waiting for transfers between devices  357 us (55%)
  local copies, waits for them, and re-layouts  95.6 us (15%)
  matrix products  86.9 us (13%)
  blocking collectives  51.2 us (8%)
  other arithmetic  44 us (7%)
  between operations  14.9 us (2%)
    psum x1, waiting for transfers between devices, broadcast(): return lax.psum(kept, axis)  175 us
    all_gather x1, waiting for transfers between devices, shards(): lax.all_gather(k_two, 'frame', axis=0, tiled=True)  99.1 us
    all_gather x1, waiting for transfers between devices, shards(): lax.all_gather(v_two, 'frame', axis=0, tiled=True)  82.9 us
    dot_general x3, matrix products, soft_step(): jnp.einsum(value_form, weights.astype(jnp.bfloat16), vals, preferred_elem...  39.1 us
    all_gather x1, blocking collectives, shards(): lax.all_gather(first_keys, 'pos', axis=0, tiled=True)  30.8 us
    reduce_sum x3, other arithmetic, soft_step(): totals = totals * keep + jnp.sum(weights, axis=-1)  27.4 us
    all_gather x1, local copies, waits for them, and re-layouts, shards(): lax.all_gather(v_one, 'pos', axis=1, tiled=True)  23.2 us
    all_gather x1, local copies, waits for them, and re-layouts, shards(): lax.all_gather(k_one, 'pos', axis=1, tiled=True)  22.5 us
  transfers between devices with their start and end apart: 5, of which 3 were waited for; matrix products, arithmetic and copies ran while one was open for 21% of the time, Pallas kernels for 0%

commit v1 on v0

--- a/solution.py
+++ b/solution.py
@@ -8,7 +8,7 @@
 
 def broadcast(value, axis, source):
     kept = jnp.where(lax.axis_index(axis) == source, value, 0).astype(value.dtype)
-    return lax.psum(kept, axis)
+    return jnp.sum(lax.all_gather(kept, axis), axis=0)
 
 
 def normed(values, gain):

time: 652 us -> 557 us (0.85)
  waiting for transfers between devices: 357 us -> 186 us
  blocking collectives: 51.2 us -> 120 us
    psum x1 -> x0, waiting for transfers between devices: 175 us -> none  [broadcast(): return lax.psum(kept, axis)]
    all_gather x0 -> x2, blocking collectives: none -> 60.8 us  [broadcast(): return jnp.sum(lax.all_gather(kept, axis), axis=0)]
  transfers between devices with their start and end apart: 5 -> 4, of which waited for: 3 -> 2; matrix products, arithmetic and copies ran while one was open for 21% -> 26% of each run, Pallas kernels for 0% -> 0%
where the time goes in v1:
time: 557 us; the launch traced here: 555 us
  waiting for transfers between devices  186 us (33%)
  blocking collectives  120 us (22%)
  local copies, waits for them, and re-layouts  97.8 us (18%)
  matrix products  92.5 us (17%)
  other arithmetic  44.6 us (8%)
  between operations  13.4 us (2%)
    all_gather x1, waiting for transfers between devices, shards(): lax.all_gather(k_two, 'frame', axis=0, tiled=True)  104 us
    all_gather x1, waiting for transfers between devices, shards(): lax.all_gather(v_two, 'frame', axis=0, tiled=True)  82.5 us
    all_gather x2, blocking collectives, broadcast(): return jnp.sum(lax.all_gather(kept, axis), axis=0)  60.8 us
    dot_general x3, matrix products, soft_step(): jnp.einsum(value_form, weights.astype(jnp.bfloat16), vals, preferred_elem...  39.1 us
    all_gather x1, blocking collectives, shards(): lax.all_gather(first_keys, 'pos', axis=0, tiled=True)  32.4 us
    reduce_sum x3, other arithmetic, soft_step(): totals = totals * keep + jnp.sum(weights, axis=-1)  27.4 us
    all_gather x1, blocking collectives, shards(): lax.all_gather(first_vals, 'pos', axis=0, tiled=True)  26.7 us
    all_gather x1, local copies, waits for them, and re-layouts, shards(): lax.all_gather(v_one, 'pos', axis=1, tiled=True)  23.2 us
  transfers between devices with their start and end apart: 4, of which 2 were waited for; matrix products, arithmetic and copies ran while one was open for 26% of the time, Pallas kernels for 0%

profile of v1, /device:TPU:1, one launch (start us, length us, event | category | flops | bytes accessed | tf_op | source)
XLA Modules:
  0.0 554.7 jit_solution(148248662649094710)
XLA Ops:
  6.5 1.6 fusion.27
  8.2 1.6 fusion.29
  9.8 2.3 convolution_convert_fusion.5
  12.1 0.0 all-gather.9.cloned.1.call-start
  12.2 1.3 convolution_convert_fusion.3
  13.5 1.5 copy.74
  15.1 0.8 slice_select_fusion.1
  15.9 31.0 %all-gather = bf16[512,256]{1,0:T(8,128)(2,1)S(1)} all-gather(bf16[64,256]{1,0:T(8,128)(2,1)S(1)} %slice_select_fusion.1), channel_id=2, replica_groups=mesh['frame'=8,'pos'=16] {'frame'}, dimensions={0}, use_global_device_ids=true | all-gather | bytes 294912 | tf_op jit(solution)/shard_map/all_gather | solution.py:11
  47.0 32.4 %all_gather.27 = bf16[1024,256]{1,0:T(8,128)(2,1)S(1)} all-gather(bf16[64,256]{1,0:T(8,128)(2,1)S(1)} %reduce_sum.76), channel_id=1, replica_groups=mesh['frame'=8,'pos'=16] {'pos'}, dimensions={0}, use_global_device_ids=true | all-gather | bytes 557056 | tf_op jit(solution)/shard_map/all_gather | solution.py:74
  79.3 1.0 copy.66
  80.3 1.4 convolution_convert_fusion.4
  81.7 3.3 reshape_reshape.6
  85.1 1.9 copy.67
  87.0 29.8 %all-gather.1 = bf16[512,256]{1,0:T(8,128)(2,1)S(1)} all-gather(bf16[64,256]{1,0:T(8,128)(2,1)S(1)} %slice_select_fusion), channel_id=3, replica_groups=mesh['frame'=8,'pos'=16] {'frame'}, dimensions={0}, use_global_device_ids=true | all-gather | bytes 294912 | tf_op jit(solution)/shard_map/all_gather | solution.py:11
  116.8 26.7 %all_gather.29 = bf16[1024,256]{1,0:T(8,128)(2,1)S(1)} all-gather(bf16[64,256]{1,0:T(8,128)(2,1)S(1)} %reduce_sum.77), channel_id=1, replica_groups=mesh['frame'=8,'pos'=16] {'pos'}, dimensions={0}, use_global_device_ids=true | all-gather | bytes 557056 | tf_op jit(solution)/shard_map/all_gather | solution.py:75
  143.5 0.2 copy.68
  143.7 18.1 %fusion.50 = f32[4,1024,2048]{1,2,0} fusion(bf16[4,64,2048]{1,2,0:T(8,128)(2,1)} %bitcast.117, bf16[1024,4,64]{0,2,1:T(8,128)(2,1)} %bitcast.124), kind=kOutput, calls=%fused_computation.75 | convolution fusion | flops 1073741824 | bytes 35127296
  161.7 12.6 %bitcast_reduce_fusion = f32[32,4,64]{2,0,1:T(8,128)S(1)} fusion(f32[4,1024,32,64]{1,3,2,0:T(8,128)} %bitcast.105), kind=kLoop, calls=%fused_computation.1 | loop fusion | flops 16769024 | bytes 33587200 | tf_op jit(solution)/shard_map/reduce_max | solution.py:34
  174.3 22.7 %copy.69 = bf16[32,1024,256]{1,2,0:T(8,128)(2,1)} copy(bf16[32,1024,256]{2,1,0:T(8,128)(2,1)} %all-gather.7.cloned.1.call-done) | data formatting | bytes 33554432 | tf_op jit(solution)/shard_map/all_gather | solution.py:82
  197.0 16.8 %multiply_reduce_fusion = (f32[32,4,64]{2,1,0:T(4,128)S(1)}, f32[32,4,64,1024]{3,2,1,0:T(8,128)}) fusion(bf16[32,1024,4,64]{1,3,2,0:T(8,128)(2,1)} %bitcast.108, bf16[32,64,4,64]{3,2,1,0:T(4,128)(2,1)S(1)} %reshape_reshape.6), kind=kOutput, calls=%fused_computation.4 | convolution fusion | flops 1090510848 | bytes 51412992 | tf_op jit(solution)/shard_map/fphd,fkhd->fhpk/dot_general | solution.py:33
  213.9 14.8 %fusion.3 = f32[32,4,64]{2,0,1:T(8,128)S(1)} fusion(f32[4,1024,32,64]{1,3,2,0:T(8,128)} %bitcast.106, f32[32,4,64]{2,0,1:T(8,128)S(1)} %get-tuple-element.13), kind=kLoop, calls=%fused_computation.7 | loop fusion | flops 25157632 | bytes 33619968 | tf_op jit(solution)/shard_map/reduce_sum | solution.py:37
  228.8 5.3 copy-done.1
  234.1 9.8 %fusion.1 = (f32[32,4,64]{2,1,0:T(4,128)S(1)}, bf16[32,4,64,1024]{3,2,1,0:T(8,128)(2,1)}) fusion(f32[32,4,64,1024]{3,2,1,0:T(8,128)S(1)} %copy-done.1, f32[32,4,64]{2,1,0:T(4,128)S(1)} %copy.73), kind=kLoop, calls=%fused_computation.5 | loop fusion | flops 33546240 | bytes 50397184 | tf_op jit(solution)/shard_map/reduce_sum | solution.py:37
  243.9 16.1 %fusion.5 = f32[4,64,32,64]{3,1,2,0:T(8,128)} fusion(bf16[1024,4,64,1]{0,2,3,1:T(8,128)(2,1)S(1)} %bitcast.123, f32[4,1024,32,64]{1,3,2,0:T(8,128)} %bitcast.107, f32[32,4,64]{2,0,1:T(8,128)S(1)} %get-tuple-element.13), kind=kOutput, calls=%fused_computation.9 | convolution fusion | flops 1098907648 | bytes 36208640 | tf_op jit(solution)/shard_map/fhpk,khd->fhpd/dot_general | solution.py:38
  260.0 23.2 %copy.75 = bf16[32,1024,256]{1,2,0:T(8,128)(2,1)} copy(bf16[32,1024,256]{2,0,1:T(8,128)(2,1)} %all-gather.9.cloned.1.call-done) | data formatting | bytes 33554432 | tf_op jit(solution)/shard_map/all_gather | solution.py:83
  283.2 15.0 %fusion.19 = bf16[32,64,4,64]{1,3,0,2:T(8,128)(2,1)} fusion(f32[4,64,32,64]{3,1,2,0:T(8,128)} %fusion.5, bf16[32,1024,4,64]{1,3,2,0:T(8,128)(2,1)} %bitcast.110, bf16[32,4,64,1024]{3,2,1,0:T(8,128)(2,1)} %get-tuple-element.8, f32[32,64,4]{1,0,2:T(8,128)S(1)} %get-tuple-element.5, f32[32,64,4]{1,0,2:T(8,128)S(1)} %get-tuple-element.6, ...), kind=kOutput, calls=%fused_computation.25 | convolution fusion | flops 1076363264 | bytes 36798464 | tf_op jit(solution)/shard_map/fhpk,fkhd->fhpd/dot_general | solution.py:38
  298.3 3.1 copy.80
  301.4 2.2 convert_element_type.78
  303.6 1.8 fusion.31
  305.4 0.9 copy-done.3
  306.3 0.3 fusion.33
  306.7 1.4 convolution_convert_fusion.1
  308.2 1.5 convolution_convert_fusion
  309.7 0.4 convolution_convert_fusion.2
  310.2 0.9 reshape_reshape.7
  311.0 103.9 %all-gather.11.cloned.1.call-done = bf16[256,64,256]{2,1,0:T(8,128)(2,1)} async-done(((bf16[32,64,256]{2,1,0:T(8,128)(2,1)}), bf16[256,64,256]{2,1,0:T(8,128)(2,1)}) %all-gather.11.cloned.1.call-update) | async-done | bytes 8388624 | tf_op jit(solution)/shard_map/all_gather | solution.py:104
  414.9 13.0 %copy.81 = bf16[256,64,256]{0,2,1:T(8,128)(2,1)} copy(bf16[256,64,256]{2,1,0:T(8,128)(2,1)} %all-gather.11.cloned.1.call-done) | data formatting | bytes 16777216 | tf_op jit(solution)/shard_map/all_gather | solution.py:104
  427.9 5.6 %multiply_reduce_fusion.1 = (f32[64,4,32]{2,1,0:T(4,128)S(1)}, f32[64,4,32,256]{3,2,1,0:T(8,128)S(1)}) fusion(bf16[256,64,4,64]{0,3,2,1:T(8,128)(2,1)} %bitcast.109, bf16[32,64,4,64]{3,2,1,0:T(4,128)(2,1)S(1)} %reshape_reshape.7), kind=kOutput, calls=%fused_computation.16 | convolution fusion | flops 272621568 | bytes 17858560 | tf_op jit(solution)/shard_map/fphd,kphd->phfk/dot_general | solution.py:33
  433.5 0.1 multiply_bitcast_fusion
  433.6 3.1 copy-done.2
  436.7 2.8 fusion.12
  439.6 0.1 bitcast_add_fusion.3
  439.7 82.5 %all-gather.13.cloned.1.call-done = bf16[256,64,256]{2,1,0:T(8,128)(2,1)} async-done(((bf16[32,64,256]{2,1,0:T(8,128)(2,1)}), bf16[256,64,256]{2,1,0:T(8,128)(2,1)}) %all-gather.13.cloned.1.call-update) | async-done | bytes 8388624 | tf_op jit(solution)/shard_map/all_gather | solution.py:105
  522.2 12.9 %copy.83 = bf16[256,64,256]{0,2,1:T(8,128)(2,1)} copy(bf16[256,64,256]{2,1,0:T(8,128)(2,1)} %all-gather.13.cloned.1.call-done) | data formatting | bytes 16777216 | tf_op jit(solution)/shard_map/all_gather | solution.py:105
  535.0 8.0 %fusion.17 = bf16[32,64,4,64]{3,0,2,1:T(8,128)(2,1)S(1)} fusion(f32[32,64,4]{0,2,1:T(4,128)S(1)} %bitcast_add_fusion.3, f32[32,64,4]{0,2,1:T(4,128)S(1)} %get-tuple-element.9, bf16[256,64,4,64]{0,3,2,1:T(8,128)(2,1)} %bitcast.118, f32[64,4,32,256]{3,2,1,0:T(8,128)} %copy-done.2, f32[64,4,32]{2,1,0:T(4,128)S(1)} %get-tuple-element.10), kind=kOutput, calls=%fused_computation.22 | convolution fusion | flops 276299776 | bytes 17924096 | tf_op jit(solution)/shard_map/phfk,kphd->phfd/dot_general | solution.py:38
  543.0 1.1 copy.84
  544.1 1.4 convert_element_type.87
  545.5 2.6 fusion.34
  (36 shorter events, 0.4 us)
Async XLA Ops:
  6.5 297.0 %copy-start = (bf16[256,256]{1,0:T(8,128)(2,1)S(1)}, bf16[256,256]{1,0:T(8,128)(2,1)}, u32[]{:S(2)}) copy-start(bf16[256,256]{1,0:T(8,128)(2,1)} %param.16) | copy-start | bytes 393220
  6.5 73.8 %copy-start.5 = (bf16[256,256]{1,0:T(8,128)(2,1)S(1)}, bf16[256,256]{1,0:T(8,128)(2,1)}, u32[]{:S(2)}) copy-start(bf16[256,256]{1,0:T(8,128)(2,1)} %param.13) | copy-start | bytes 393220
  6.5 167.8 %all-gather.7.cloned.1.call-start = ((), (), s32[]{:S(2)}) async-start(), calls=%async_computation | async-start | bytes 17825792 | tf_op jit(solution)/shard_map/all_gather | solution.py:82
  12.1 247.9 %all-gather.9.cloned.1.call-start = ((), (), s32[]{:S(2)}) async-start(), calls=%async_computation.1 | async-start | bytes 17825792 | tf_op jit(solution)/shard_map/all_gather | solution.py:83
  15.1 399.8 %all-gather.11.cloned.1.call-start = ((), (), s32[]{:S(2)}) async-start(), calls=%async_computation.2 | async-start | bytes 9437184 | tf_op jit(solution)/shard_map/all_gather | solution.py:104
  213.9 20.2 %copy-start.1 = (f32[32,4,64,1024]{3,2,1,0:T(8,128)S(1)}, f32[32,4,64,1024]{3,2,1,0:T(8,128)}, u32[]{:S(2)}) copy-start(f32[32,4,64,1024]{3,2,1,0:T(8,128)} %get-tuple-element.15) | copy-start | bytes 100663296
  283.2 20.3 %copy-start.4 = (bf16[32,64,256]{2,1,0:T(8,128)(2,1)S(1)}, bf16[32,64,256]{2,1,0:T(8,128)(2,1)}, u32[]{:S(2)}) copy-start(bf16[32,64,256]{2,1,0:T(8,128)(2,1)} %param.11) | copy-start | bytes 3145732
  298.3 8.1 %copy-start.10 = (f32[256]{0:T(256)S(1)}, f32[256]{0:T(256)}, u32[]{:S(2)}) copy-start(f32[256]{0:T(256)} %param.17) | copy-start | bytes 3076
  298.3 8.4 %copy-start.6 = (bf16[256,256]{1,0:T(8,128)(2,1)S(1)}, bf16[256,256]{1,0:T(8,128)(2,1)}, u32[]{:S(2)}) copy-start(bf16[256,256]{1,0:T(8,128)(2,1)} %param.19) | copy-start | bytes 393220
  298.3 9.9 %copy-start.7 = (bf16[256,256]{1,0:T(8,128)(2,1)S(1)}, bf16[256,256]{1,0:T(8,128)(2,1)}, u32[]{:S(2)}) copy-start(bf16[256,256]{1,0:T(8,128)(2,1)} %param.20) | copy-start | bytes 393220
  303.6 6.2 %copy-start.8 = (bf16[256,256]{1,0:T(8,128)(2,1)S(1)}, bf16[256,256]{1,0:T(8,128)(2,1)}, u32[]{:S(2)}) copy-start(bf16[256,256]{1,0:T(8,128)(2,1)} %param.18) | copy-start | bytes 393220
  305.4 1.0 copy-start.3
  308.2 214.0 %all-gather.13.cloned.1.call-start = ((), (), s32[]{:S(2)}) async-start(), calls=%async_computation.3 | async-start | bytes 9437184 | tf_op jit(solution)/shard_map/all_gather | solution.py:105
  433.5 3.2 copy-start.2
  535.0 10.5 %copy-start.9 = (bf16[256,256]{1,0:T(8,128)(2,1)S(1)}, bf16[256,256]{1,0:T(8,128)(2,1)}, u32[]{:S(2)}) copy-start(bf16[256,256]{1,0:T(8,128)(2,1)} %param.21) | copy-start | bytes 393220
Sparse Core Ops, SparseCore 0:
  12.2 104.1 all-gather.6
  118.1 93.8 all-gather.8
  308.3 106.5 all-gather.10
  417.1 105.0 all-gather.12
